TPU v7x, 128 devices: a whole 4x4x4 slice. The times are simulated.
128 devices in a mesh: row: 4 (over y_hi, core), col: 32 (over x, z, y_lo).
Axes of the slice: x: 4, y: 4 (y_hi: 2, y_lo: 2; y = y_hi * 2 + y_lo), z: 4, core: 2. Of those that a mesh axis runs over, the one named last changes fastest.
Arguments:
- inputs: bfloat16 [1024, 8192], P(('row', 'col')), may hold values from -6 to 6
- layer_norm_gain: float32 [8192], replicated, may hold values from 0.1 to 1.9
- w_in: bfloat16 [8192, 16384], P('row', 'col'), may hold values from -0.09375 to 0.09375
- w_out: bfloat16 [16384, 8192], P('col', 'row'), may hold values from -0.0625 to 0.0625
- pattern_in: int32 [64, 16], replicated, may hold values from 0 to 31, as said below
- pattern_out: int32 [32, 32], replicated, may hold values from 0 to 63, as said below
- out_grad: bfloat16 [1024, 8192], P(('row', 'col')), may hold values from -6 to 6
Outputs:
- output: bfloat16 [1024, 8192], P(('row', 'col'))
- grad_inputs: bfloat16 [1024, 8192], P(('row', 'col'))
- grad_w_in: bfloat16 [8192, 16384], P('row', 'col')
- grad_w_out: bfloat16 [16384, 8192], P('col', 'row')
- norm_gain_gradient: float32 [8192], replicated
Inputs may be any that keep to these rules, and one draw needn't show every extreme that they name: `pattern_in`: each row lists 8192 / 512 different tile rows in increasing order. `pattern_out`: each row lists 16384 / 512 different tile rows in increasing order.
All inputs are finite; a program needn't handle non-finite values.
Results may differ from a plain program's by a relative error of at most 0.022.
Values may be sent and summed in bfloat16 or wider, within the bound.
A program may use at most 128 MiB of HBM per device.

v0:
```python
import jax
import jax.numpy as jnp
from jax import lax
from jax.sharding import PartitionSpec as P

D = 8192
FF = 16384
BLOCK = 256


def cut_along(shard, dim, count):
    before, after = (shard.shape[:dim], shard.shape[dim + 1 :])
    return jnp.moveaxis(shard.reshape(*before, count, -1, *after), dim, 0)


def sum_at_owner(shard, axis, dim):
    pieces = cut_along(shard, dim, lax.axis_size(axis))
    arrived = lax.all_to_all(pieces, axis, split_axis=0, concat_axis=0, tiled=True)
    return arrived.astype(jnp.float32).sum(axis=0)


def block_mask(pattern, tile_rows):
    iota = jnp.arange(tile_rows, dtype=jnp.int32)
    return jnp.any(pattern[None, :, :] == iota[:, None, None], axis=2)


def apply_mask(weight, mask):
    rows_t, cols_t = mask.shape
    shaped = weight.reshape(rows_t, BLOCK, cols_t, BLOCK)
    kept = jnp.where(mask[:, None, :, None], shaped, jnp.zeros((), weight.dtype))
    return kept.reshape(weight.shape)


def gelu_value(h):
    inner = 0.7978845608 * (h + 0.044715 * h * h * h)
    return 0.5 * h * (1.0 + jnp.tanh(inner))


def gelu_slope(h):
    tanh_v = jnp.tanh(0.7978845608 * (h + 0.044715 * h * h * h))
    return 0.5 * (1.0 + tanh_v) + 0.5 * h * (1.0 - tanh_v * tanh_v) * 0.7978845608 * (
        1.0 + 0.134145 * h * h
    )


def dot_last(left, right):
    return lax.dot_general(
        left, right, (((1,), (1,)), ((), ())), preferred_element_type=jnp.float32
    )


def dot_first(left, right):
    return lax.dot_general(
        left, right, (((0,), (0,)), ((), ())), preferred_element_type=jnp.float32
    )


def shards(inputs, layer_norm_gain, w_in, w_out, pattern_in, pattern_out, out_grad):
    n_row = lax.axis_size("row")
    n_col = lax.axis_size("col")
    row_index = lax.axis_index("row")
    col_index = lax.axis_index("col")
    tok_here = inputs.shape[0]
    feat_tiles = w_in.shape[0] // BLOCK
    unit_tiles = w_in.shape[1] // BLOCK
    mask_in = lax.dynamic_slice(
        block_mask(pattern_in, D // BLOCK),
        (row_index * feat_tiles, col_index * unit_tiles),
        (feat_tiles, unit_tiles),
    )
    mask_out = lax.dynamic_slice(
        block_mask(pattern_out, FF // BLOCK),
        (col_index * unit_tiles, row_index * feat_tiles),
        (unit_tiles, feat_tiles),
    )
    w_in_e = apply_mask(w_in, mask_in)
    w_out_e = apply_mask(w_out, mask_out)
    xfloat = inputs.astype(jnp.float32)
    centered_input = xfloat - jnp.mean(xfloat, axis=1, keepdims=True)
    inverse_deviation = lax.rsqrt(
        jnp.mean(centered_input * centered_input, axis=1, keepdims=True) + 1e-05
    )
    standardized_input = centered_input * inverse_deviation
    normalized_input = (standardized_input * layer_norm_gain[None, :]).astype(jnp.bfloat16)
    swapped = lax.all_to_all(normalized_input, "row", split_axis=1, concat_axis=0, tiled=True)
    allrows = lax.all_gather(swapped, "col", axis=0, tiled=True)
    slice_width = allrows.shape[1]
    byrow = (
        allrows.reshape(n_col, n_row, tok_here, slice_width)
        .transpose(1, 0, 2, 3)
        .reshape(-1, slice_width)
    )
    hidden_pre = lax.psum_scatter(
        jnp.dot(byrow, w_in_e, preferred_element_type=jnp.float32).astype(jnp.bfloat16),
        "row",
        scatter_dimension=0,
        tiled=True,
    ).astype(jnp.float32)
    activation = gelu_value(hidden_pre).astype(jnp.bfloat16)
    w_out_full = lax.all_gather(w_out_e, "row", axis=1, tiled=True)
    summed = sum_at_owner(
        jnp.dot(activation, w_out_full, preferred_element_type=jnp.float32).astype(jnp.bfloat16),
        "col",
        0,
    )
    output = (xfloat + summed).astype(jnp.bfloat16)
    grad_panel = lax.all_gather(out_grad, "col", axis=0, tiled=True)
    d_act = dot_last(grad_panel, w_out_full)
    d_pre = (d_act * gelu_slope(hidden_pre)).astype(jnp.bfloat16)
    w2_sum = lax.psum_scatter(
        dot_first(activation, grad_panel).astype(jnp.bfloat16),
        "row",
        scatter_dimension=1,
        tiled=True,
    )
    grad_w_out = apply_mask(w2_sum, mask_out)
    d_all = lax.all_gather(d_pre, "row", axis=0, tiled=True)
    unit_width = d_all.shape[1]
    panel_terms = jnp.einsum(
        "gtf,gth->gfh",
        byrow.reshape(n_row, -1, slice_width),
        d_all.reshape(n_row, -1, unit_width),
        preferred_element_type=jnp.float32,
    )
    panel_rounded = lax.optimization_barrier(panel_terms.astype(jnp.bfloat16))
    w1_sum = jnp.sum(panel_rounded.astype(jnp.float32), axis=0)
    d_order = (
        d_all.reshape(n_row, n_col, tok_here, unit_width)
        .transpose(1, 0, 2, 3)
        .reshape(-1, unit_width)
    )
    slices = sum_at_owner(dot_last(d_order, w_in_e).astype(jnp.bfloat16), "col", 0)
    normed_gradient = lax.all_to_all(
        slices.astype(jnp.bfloat16), "row", split_axis=0, concat_axis=1, tiled=True
    ).astype(slices.dtype)
    grad_w_in = apply_mask(w1_sum.astype(jnp.bfloat16), mask_in)
    norm_gain_gradient = lax.psum(
        jnp.sum(normed_gradient * standardized_input, axis=0), ("row", "col")
    )
    gain_scaled = normed_gradient * layer_norm_gain[None, :]
    backward_result = inverse_deviation * (
        gain_scaled
        - jnp.mean(gain_scaled, axis=1, keepdims=True)
        - standardized_input * jnp.mean(gain_scaled * standardized_input, axis=1, keepdims=True)
    )
    grad_inputs = (out_grad.astype(jnp.float32) + backward_result).astype(jnp.bfloat16)
    return (output, grad_inputs, grad_w_in, grad_w_out, norm_gain_gradient)


def solution(mesh):
    in_specs = (
        P(("row", "col"), None),
        P(),
        P("row", "col"),
        P("col", "row"),
        P(),
        P(),
        P(("row", "col"), None),
    )
    out_specs = (
        P(("row", "col"), None),
        P(("row", "col"), None),
        P("row", "col"),
        P("col", "row"),
        P(),
    )
    return jax.shard_map(shards, mesh=mesh, in_specs=in_specs, out_specs=out_specs, check_vma=False)
```

profile of v0, /device:TPU:1, one launch (start us, length us, event | category | flops | bytes accessed | tf_op | source)
XLA Modules:
  0.0 768.9 jit_solution(16966023902262134158)
XLA Ops:
  7.2 1.1 convert_reduce_fusion.1
  8.3 1.2 fusion.27
  9.5 1.0 fusion.20
  10.5 10.9 %all_to_all.42 = bf16[8,4,2048]{2,0,1:T(8,128)(2,1)} all-to-all(bf16[8,4,2048]{2,0,1:T(8,128)(2,1)S(1)} %bitcast.58), channel_id=1, replica_groups=mesh['row'=4,'col'=32] {'row'}, dimensions={1} | all-to-all | bytes 262144 | tf_op jit(solution)/shard_map/all_to_all | solution.py:85
  21.5 0.7 all-gather.9.cloned.1.call-update
  22.2 0.8 fusion.29
  23.0 0.1 dynamic_slice.6
  23.1 0.1 copy.31
  23.2 0.3 broadcast_in_dim.50
  23.5 0.6 copy.41
  24.2 1.2 copy.32
  25.4 132.9 %all-gather.5.cloned.1.call-done = bf16[1024,2048]{1,0:T(8,128)(2,1)} async-done(((bf16[32,2048]{1,0:T(8,128)(2,1)}), bf16[1024,2048]{1,0:T(8,128)(2,1)}) %all-gather.5.cloned.1.call-update) | async-done | bytes 4194320 | tf_op jit(solution)/shard_map/all_gather | solution.py:86
  158.2 2.6 copy.30
  160.9 0.2 copy-done.6
  161.1 3.4 convolution_convert_fusion.4
  164.5 152.4 %all-gather.9.cloned.1.call-done = bf16[256,8192]{1,0:T(8,128)(2,1)} async-done(((bf16[8,8192]{1,0:T(8,128)(2,1)}), bf16[256,8192]{1,0:T(8,128)(2,1)}) %all-gather.9.cloned.1.call-update) | async-done | bytes 4194320 | tf_op jit(solution)/shard_map/all_gather | solution.py:107
  316.9 55.4 %reduce-scatter.3.cloned.1.call-done = bf16[256,512]{1,0:T(8,128)(2,1)} async-done(((bf16[1024,512]{1,0:T(8,128)(2,1)}), bf16[256,512]{1,0:T(8,128)(2,1)}) %reduce-scatter.3.cloned.1.call-update) | async-done | bytes 262160 | tf_op jit(solution)/shard_map/reduce_scatter | solution.py:93
  372.3 8.0 %convolution_convert_fusion = bf16[512,8192]{1,0:T(8,128)(2,1)} fusion(bf16[256,8192]{1,0:T(8,128)(2,1)} %all-gather.9.cloned.1.call-done, bf16[256,512]{1,0:T(8,128)(2,1)} %reduce-scatter.3.cloned.1.call-done), kind=kOutput, calls=%fused_computation | convolution fusion | flops 2152988672 | bytes 12845056 | tf_op jit(solution)/shard_map/dot_general | solution.py:53
  380.4 0.6 copy-done.5
  381.1 0.2 fusion.13
  381.3 0.1 dynamic_slice.7
  381.4 0.1 copy.33
  381.5 0.3 broadcast_in_dim.53
  381.8 0.6 copy.42
  382.5 75.6 %reduce-scatter.5.cloned.1.call-done = bf16[512,2048]{1,0:T(8,128)(2,1)} async-done(((bf16[512,8192]{1,0:T(8,128)(2,1)}), bf16[512,2048]{1,0:T(8,128)(2,1)}) %reduce-scatter.5.cloned.1.call-update) | async-done | bytes 2097168 | tf_op jit(solution)/shard_map/reduce_scatter | solution.py:110
  458.1 4.6 broadcast_select_fusion
  462.8 0.2 all-gather.11.cloned.1.call-start
  463.0 62.2 %all-gather.7.cloned.1.call-done = bf16[512,8192]{1,0:T(8,128)(2,1)} async-done(((bf16[512,2048]{1,0:T(8,128)(2,1)}), bf16[512,8192]{1,0:T(8,128)(2,1)}) %all-gather.7.cloned.1.call-update) | async-done | bytes 8388624 | tf_op jit(solution)/shard_map/all_gather | solution.py:100
  525.2 7.8 %fusion.3 = bf16[256,512]{1,0:T(8,128)(2,1)} fusion(bf16[512,8192]{1,0:T(8,128)(2,1)} %all-gather.7.cloned.1.call-done, bf16[256,8192]{1,0:T(8,128)(2,1)} %all-gather.9.cloned.1.call-done, bf16[256,512]{1,0:T(8,128)(2,1)S(1)} %copy-done.4), kind=kOutput, calls=%fused_computation.17 | convolution fusion | flops 2150105088 | bytes 13107200 | tf_op jit(solution)/shard_map/dot_general | solution.py:47
  533.1 20.3 %all-gather.11.cloned.1.call-done = bf16[1024,512]{1,0:T(8,128)(2,1)} async-done(((bf16[256,512]{1,0:T(8,128)(2,1)}), bf16[1024,512]{1,0:T(8,128)(2,1)}) %all-gather.11.cloned.1.call-update) | async-done | bytes 1048592 | tf_op jit(solution)/shard_map/all_gather | solution.py:117
  553.4 1.3 copy.35
  554.7 6.0 convolution_convert_fusion.3
  560.7 7.1 all-to-all-start.2
  567.8 7.7 %fusion = bf16[32,8,8192]{2,1,0:T(8,128)(2,1)} fusion(bf16[512,8192]{1,0:T(8,128)(2,1)} %all-gather.7.cloned.1.call-done, bf16[256,512]{1,0:T(8,128)(2,1)S(1)} %copy-done.4), kind=kOutput, calls=%fused_computation.2 | convolution fusion | flops 2150891520 | bytes 12845056 | tf_op jit(solution)/shard_map/dot_general | solution.py:102
  575.5 46.5 %all-to-all-done.2 = bf16[32,32,2048]{2,1,0:T(8,128)(2,1)} async-done(((bf16[32,32,2048]{2,1,0:T(8,128)(2,1)}), bf16[32,32,2048]{2,1,0:T(8,128)(2,1)}, u32[]{:S(2)}, u32[]{:S(2)}) %all-to-all-start.2) | async-done | bytes 4194336 | tf_op jit(solution)/shard_map/all_to_all | solution.py:18
  622.0 10.2 %all-to-all-start.1 = ((bf16[32,8,8192]{2,1,0:T(8,128)(2,1)}), bf16[32,8,8192]{2,1,0:T(8,128)(2,1)}, u32[]{:S(2)}, u32[]{:S(2)}) async-start(bf16[32,8,8192]{2,1,0:T(8,128)(2,1)} %fusion), calls=%async_computation.2 | async-start | bytes 8388608 | tf_op jit(solution)/shard_map/all_to_all | solution.py:18
  632.3 7.8 %convolution_convert_fusion.2 = bf16[4,2048,512]{2,1,0:T(8,128)(2,1)} fusion(bf16[4,256,512]{2,1,0:T(8,128)(2,1)S(1)} %bitcast.53, bf16[4,32,8,2048]{3,2,0,1:T(8,128)(2,1)} %bitcast.45), kind=kOutput, calls=%fused_computation.4 | convolution fusion | flops 2151677952 | bytes 13631488 | tf_op jit(solution)/shard_map/gtf,gth->gfh/dot_general | solution.py:119
  640.1 6.1 reduce_sum.84
  646.2 1.8 broadcast_select_fusion.2
  648.0 3.7 reduce_sum.81
  651.7 33.6 %all-to-all-done.1 = bf16[32,8,8192]{2,1,0:T(8,128)(2,1)} async-done(((bf16[32,8,8192]{2,1,0:T(8,128)(2,1)}), bf16[32,8,8192]{2,1,0:T(8,128)(2,1)}, u32[]{:S(2)}, u32[]{:S(2)}) %all-to-all-start.1) | async-done | bytes 4194336 | tf_op jit(solution)/shard_map/all_to_all | solution.py:18
  685.3 5.7 all-to-all-start.3
  691.0 2.8 convert_reduce_fusion
  693.8 2.3 all-to-all-done.3
  696.1 0.2 multiply_reduce_fusion
  696.3 0.3 fusion.26
  696.6 64.7 %psum.7 = f32[8192]{0:T(1024)} all-reduce(f32[8192]{0:T(1024)S(1)} %get-tuple-element.10), channel_id=1, replica_groups=mesh['row'=4,'col'=32] {'row','col'}, use_global_device_ids=true, to_apply=%region_12.13 | all-reduce | flops 8192 | bytes 65536 | tf_op jit(solution)/shard_map/psum | solution.py:137
  761.3 0.8 fusion.25
  (28 shorter events, 0.4 us)
Async XLA Ops:
  7.2 151.1 %all-gather.5.cloned.1.call-start = ((), (), s32[]{:S(2)}) async-start(), calls=%async_computation.6 | async-start | bytes 4325376 | tf_op jit(solution)/shard_map/all_gather | solution.py:86
  21.4 295.5 %all-gather.9.cloned.1.call-start = ((), (), s32[]{:S(2)}) async-start(), calls=%async_computation.9 | async-start | bytes 4325376 | tf_op jit(solution)/shard_map/all_gather | solution.py:107
  22.2 350.1 %reduce-scatter.3.cloned.1.call-start = ((), (), s32[]{:S(2)}) async-start(), calls=%async_computation.7 | async-start | bytes 1310720 | tf_op jit(solution)/shard_map/reduce_scatter | solution.py:93
  158.2 2.9 copy-start.6
  164.5 293.6 %reduce-scatter.5.cloned.1.call-start = ((), (), s32[]{:S(2)}) async-start(), calls=%async_computation.11 | async-start | bytes 10485760 | tf_op jit(solution)/shard_map/reduce_scatter | solution.py:110
  380.4 0.7 copy-start.5
  380.4 144.8 %all-gather.7.cloned.1.call-start = ((), (), s32[]{:S(2)}) async-start(), calls=%async_computation.8 | async-start | bytes 10485760 | tf_op jit(solution)/shard_map/all_gather | solution.py:100
  458.1 67.1 %copy-start.4 = (bf16[256,512]{1,0:T(8,128)(2,1)S(1)}, bf16[256,512]{1,0:T(8,128)(2,1)}, u32[]{:S(2)}) copy-start(bf16[256,512]{1,0:T(8,128)(2,1)} %reduce-scatter.3.cloned.1.call-done) | copy-start | bytes 786436
  462.8 90.6 %all-gather.11.cloned.1.call-start = ((), (), s32[]{:S(2)}) async-start(), calls=%async_computation.10 | async-start | bytes 1310720 | tf_op jit(solution)/shard_map/all_gather | solution.py:117
  560.7 61.4 %all-to-all-start.2 = ((bf16[32,32,2048]{2,1,0:T(8,128)(2,1)}), bf16[32,32,2048]{2,1,0:T(8,128)(2,1)}, u32[]{:S(2)}, u32[]{:S(2)}) async-start(bf16[32,32,2048]{2,1,0:T(8,128)(2,1)} %bitcast.47), calls=%async_computation.3 | async-start | bytes 8388608 | tf_op jit(solution)/shard_map/all_to_all | solution.py:18
  575.5 56.7 %copy-start.2 = (f32[8192]{0:T(1024)S(1)}, f32[8192]{0:T(1024)}, u32[]{:S(2)}) copy-start(f32[8192]{0:T(1024)} %param.8) | copy-start | bytes 98308
  575.5 56.7 %copy-start = (bf16[1024,512]{1,0:T(8,128)(2,1)S(1)}, bf16[1024,512]{1,0:T(8,128)(2,1)}, u32[]{:S(2)}) copy-start(bf16[1024,512]{1,0:T(8,128)(2,1)} %all-gather.11.cloned.1.call-done) | copy-start | bytes 3145732
  622.0 63.3 %all-to-all-start.1 = ((bf16[32,8,8192]{2,1,0:T(8,128)(2,1)}), bf16[32,8,8192]{2,1,0:T(8,128)(2,1)}, u32[]{:S(2)}, u32[]{:S(2)}) async-start(bf16[32,8,8192]{2,1,0:T(8,128)(2,1)} %fusion), calls=%async_computation.2 | async-start | bytes 8388608 | tf_op jit(solution)/shard_map/all_to_all | solution.py:18
  648.0 48.3 %copy-start.1 = (bf16[8,8192]{1,0:T(8,128)(2,1)S(1)}, bf16[8,8192]{1,0:T(8,128)(2,1)}, u32[]{:S(2)}) copy-start(bf16[8,8192]{1,0:T(8,128)(2,1)} %param.7) | copy-start | bytes 393220
  648.0 113.3 %copy-start.3 = (bf16[8,8192]{1,0:T(8,128)(2,1)S(1)}, bf16[8,8192]{1,0:T(8,128)(2,1)}, u32[]{:S(2)}) copy-start(bf16[8,8192]{1,0:T(8,128)(2,1)} %param.13) | copy-start | bytes 393220
  685.3 10.8 %all-to-all-start.3 = ((bf16[4,8,2048]{2,1,0:T(8,128)(2,1)}), bf16[4,8,2048]{2,1,0:T(8,128)(2,1)S(1)}, u32[]{:S(2)}, u32[]{:S(2)}) async-start(bf16[4,8,2048]{2,1,0:T(8,128)(2,1)} %bitcast.12), calls=%async_computation.4 | async-start | bytes 262144 | tf_op jit(solution)/shard_map/all_to_all | solution.py:133
Sparse Core Ops, SparseCore 0:
  21.6 136.6 all-gather.4
  159.9 157.0 all-gather.8
  320.1 52.1 reduce-scatter.2
  380.5 77.5 reduce-scatter.4
  462.9 62.2 all-gather.6
  533.2 20.1 all-gather.10
where the time goes:
time: 770 us; the launch traced here: 769 us
  waiting for transfers between devices  582 us (76%)
  blocking collectives  75.6 us (10%)
  matrix products  40.8 us (5%)
  other arithmetic  24.6 us (3%)
  starting transfers between devices  23.4 us (3%)
  between operations  14.2 us (2%)
  local copies, waits for them, and re-layouts  8.34 us (1%)
    all_gather x1, waiting for transfers between devices, shards(): grad_panel = lax.all_gather(out_grad, 'col', axis=0, tiled=True)  152 us
    all_gather x1, waiting for transfers between devices, shards(): allrows = lax.all_gather(swapped, 'col', axis=0, tiled=True)  133 us
    all_to_all x2, waiting for transfers between devices, sum_at_owner(): lax.all_to_all(pieces, axis, split_axis=0, concat_axis=0, tiled=True)  80.1 us
    reduce_scatter x1, waiting for transfers between devices, shards(): lax.psum_scatter(dot_first(activation, grad_panel).astype(jnp.bfloat16),...  75.6 us
    psum x1, blocking collectives, shards(): lax.psum(jnp.sum(normed_gradient * standardized_input, axis=0), ('row', '...  64.7 us
    all_gather x1, waiting for transfers between devices, shards(): w_out_full = lax.all_gather(w_out_e, 'row', axis=1, tiled=True)  62.2 us
    reduce_scatter x1, waiting for transfers between devices, shards(): lax.psum_scatter(jnp.dot(byrow, w_in_e, preferred_element_type=jnp.float3...  55.4 us
    all_gather x1, waiting for transfers between devices, shards(): d_all = lax.all_gather(d_pre, 'row', axis=0, tiled=True)  20.3 us
  transfers between devices with their start and end apart: 9, of which 9 were waited for; matrix products, arithmetic and copies ran while one was open for 5% of the time, Pallas kernels for 0%

commit v1 on v0

--- a/solution.py
+++ b/solution.py
@@ -134,9 +134,8 @@
         slices.astype(jnp.bfloat16), "row", split_axis=0, concat_axis=1, tiled=True
     ).astype(slices.dtype)
     grad_w_in = apply_mask(w1_sum.astype(jnp.bfloat16), mask_in)
-    norm_gain_gradient = lax.psum(
-        jnp.sum(normed_gradient * standardized_input, axis=0), ("row", "col")
-    )
+    half = lax.psum(jnp.sum(normed_gradient * standardized_input, axis=0), "col")
+    norm_gain_gradient = lax.psum(half, "row")
     gain_scaled = normed_gradient * layer_norm_gain[None, :]
     backward_result = inverse_deviation * (
         gain_scaled

time: 770 us -> 874 us (1.14)
  blocking collectives: 75.6 us -> 180 us
    psum x1 -> x2, blocking collectives: 64.7 us -> 169 us  [the longest x1 128 us: shards(): lax.psum(jnp.sum(normed_gradient * standardized_input, axis=0), 'col')]
where the time goes in v1:
time: 874 us
  waiting for transfers between devices  582 us (67%)
  blocking collectives  180 us (21%)
  matrix products  40.8 us (5%)
  other arithmetic  24.6 us (3%)
  starting transfers between devices  23.4 us (3%)
  between operations  14.2 us (2%)
    all_gather x1, waiting for transfers between devices, shards(): grad_panel = lax.all_gather(out_grad, 'col', axis=0, tiled=True)  152 us
    all_gather x1, waiting for transfers between devices, shards(): allrows = lax.all_gather(swapped, 'col', axis=0, tiled=True)  133 us
    psum x1, blocking collectives, shards(): lax.psum(jnp.sum(normed_gradient * standardized_input, axis=0), 'col')  128 us
    all_to_all x2, waiting for transfers between devices, sum_at_owner(): lax.all_to_all(pieces, axis, split_axis=0, concat_axis=0, tiled=True)  80.1 us
    reduce_scatter x1, waiting for transfers between devices, shards(): lax.psum_scatter(dot_first(activation, grad_panel).astype(jnp.bfloat16),...  75.6 us
    all_gather x1, waiting for transfers between devices, shards(): w_out_full = lax.all_gather(w_out_e, 'row', axis=1, tiled=True)  62.2 us
    reduce_scatter x1, waiting for transfers between devices, shards(): lax.psum_scatter(jnp.dot(byrow, w_in_e, preferred_element_type=jnp.float3...  55.4 us
    psum x1, blocking collectives, shards(): norm_gain_gradient = lax.psum(half, 'row')  41.7 us
  transfers between devices with their start and end apart: 9, of which 9 were waited for; matrix products, arithmetic and copies ran while one was open for 5% of the time, Pallas kernels for 0%

profile of v1, /device:TPU:1, one launch (start us, length us, event | category | flops | bytes accessed | tf_op | source)
XLA Modules:
  0.0 873.6 jit_solution(6108246785835649484)
XLA Ops:
  7.2 1.1 convert_reduce_fusion.1
  8.3 1.2 fusion.27
  9.5 1.0 fusion.20
  10.5 10.9 %all_to_all.42 = bf16[8,4,2048]{2,0,1:T(8,128)(2,1)} all-to-all(bf16[8,4,2048]{2,0,1:T(8,128)(2,1)S(1)} %bitcast.58), channel_id=1, replica_groups=mesh['row'=4,'col'=32] {'row'}, dimensions={1} | all-to-all | bytes 262144 | tf_op jit(solution)/shard_map/all_to_all | solution.py:85
  21.5 0.7 all-gather.9.cloned.1.call-update
  22.2 0.8 fusion.29
  23.0 0.1 dynamic_slice.6
  23.1 0.1 copy.31
  23.2 0.3 broadcast_in_dim.50
  23.5 0.6 copy.41
  24.2 1.2 copy.32
  25.4 132.9 %all-gather.5.cloned.1.call-done = bf16[1024,2048]{1,0:T(8,128)(2,1)} async-done(((bf16[32,2048]{1,0:T(8,128)(2,1)}), bf16[1024,2048]{1,0:T(8,128)(2,1)}) %all-gather.5.cloned.1.call-update) | async-done | bytes 4194320 | tf_op jit(solution)/shard_map/all_gather | solution.py:86
  158.2 2.6 copy.30
  160.9 0.2 copy-done.6
  161.1 3.4 convolution_convert_fusion.4
  164.5 152.4 %all-gather.9.cloned.1.call-done = bf16[256,8192]{1,0:T(8,128)(2,1)} async-done(((bf16[8,8192]{1,0:T(8,128)(2,1)}), bf16[256,8192]{1,0:T(8,128)(2,1)}) %all-gather.9.cloned.1.call-update) | async-done | bytes 4194320 | tf_op jit(solution)/shard_map/all_gather | solution.py:107
  316.9 55.4 %reduce-scatter.3.cloned.1.call-done = bf16[256,512]{1,0:T(8,128)(2,1)} async-done(((bf16[1024,512]{1,0:T(8,128)(2,1)}), bf16[256,512]{1,0:T(8,128)(2,1)}) %reduce-scatter.3.cloned.1.call-update) | async-done | bytes 262160 | tf_op jit(solution)/shard_map/reduce_scatter | solution.py:93
  372.3 8.0 convolution_convert_fusion
  380.4 0.6 copy-done.5
  381.1 0.2 fusion.13
  381.4 0.1 copy.33
  381.5 0.3 broadcast_in_dim.53
  381.8 0.6 copy.42
  382.5 75.6 %reduce-scatter.5.cloned.1.call-done = bf16[512,2048]{1,0:T(8,128)(2,1)} async-done(((bf16[512,8192]{1,0:T(8,128)(2,1)}), bf16[512,2048]{1,0:T(8,128)(2,1)}) %reduce-scatter.5.cloned.1.call-update) | async-done | bytes 2097168 | tf_op jit(solution)/shard_map/reduce_scatter | solution.py:110
  458.1 4.6 broadcast_select_fusion
  462.8 0.2 all-gather.11.cloned.1.call-start
  463.0 62.2 %all-gather.7.cloned.1.call-done = bf16[512,8192]{1,0:T(8,128)(2,1)} async-done(((bf16[512,2048]{1,0:T(8,128)(2,1)}), bf16[512,8192]{1,0:T(8,128)(2,1)}) %all-gather.7.cloned.1.call-update) | async-done | bytes 8388624 | tf_op jit(solution)/shard_map/all_gather | solution.py:100
  525.2 7.8 fusion.3
  533.1 20.3 %all-gather.11.cloned.1.call-done = bf16[1024,512]{1,0:T(8,128)(2,1)} async-done(((bf16[256,512]{1,0:T(8,128)(2,1)}), bf16[1024,512]{1,0:T(8,128)(2,1)}) %all-gather.11.cloned.1.call-update) | async-done | bytes 1048592 | tf_op jit(solution)/shard_map/all_gather | solution.py:117
  553.4 1.3 copy.35
  554.7 6.0 convolution_convert_fusion.3
  560.7 7.1 all-to-all-start.2
  567.8 7.7 fusion
  575.5 46.5 %all-to-all-done.2 = bf16[32,32,2048]{2,1,0:T(8,128)(2,1)} async-done(((bf16[32,32,2048]{2,1,0:T(8,128)(2,1)}), bf16[32,32,2048]{2,1,0:T(8,128)(2,1)}, u32[]{:S(2)}, u32[]{:S(2)}) %all-to-all-start.2) | async-done | bytes 4194336 | tf_op jit(solution)/shard_map/all_to_all | solution.py:18
  622.0 10.2 %all-to-all-start.1 = ((bf16[32,8,8192]{2,1,0:T(8,128)(2,1)}), bf16[32,8,8192]{2,1,0:T(8,128)(2,1)}, u32[]{:S(2)}, u32[]{:S(2)}) async-start(bf16[32,8,8192]{2,1,0:T(8,128)(2,1)} %fusion), calls=%async_computation.2 | async-start | bytes 8388608 | tf_op jit(solution)/shard_map/all_to_all | solution.py:18
  632.3 7.8 convolution_convert_fusion.2
  640.1 6.1 reduce_sum.84
  646.2 1.8 broadcast_select_fusion.2
  648.0 3.7 reduce_sum.81
  651.7 33.6 %all-to-all-done.1 = bf16[32,8,8192]{2,1,0:T(8,128)(2,1)} async-done(((bf16[32,8,8192]{2,1,0:T(8,128)(2,1)}), bf16[32,8,8192]{2,1,0:T(8,128)(2,1)}, u32[]{:S(2)}, u32[]{:S(2)}) %all-to-all-start.1) | async-done | bytes 4194336 | tf_op jit(solution)/shard_map/all_to_all | solution.py:18
  685.3 5.7 all-to-all-start.3
  691.0 2.8 convert_reduce_fusion
  693.8 2.3 all-to-all-done.3
  696.1 0.2 multiply_reduce_fusion
  696.3 0.3 fusion.26
  696.6 127.6 %psum.14 = f32[8192]{0:T(1024)S(1)} all-reduce(f32[8192]{0:T(1024)S(1)} %get-tuple-element.10), channel_id=1, replica_groups=mesh['row'=4,'col'=32] {'col'}, use_global_device_ids=true, to_apply=%region_12.13 | all-reduce | flops 8192 | bytes 65536 | tf_op jit(solution)/shard_map/psum | solution.py:137
  824.2 41.7 %psum.15 = f32[8192]{0:T(1024)} all-reduce(f32[8192]{0:T(1024)S(1)} %psum.14), channel_id=1, replica_groups=mesh['row'=4,'col'=32] {'row'}, use_global_device_ids=true, to_apply=%region_13.14 | all-reduce | flops 8192 | bytes 65536 | tf_op jit(solution)/shard_map/psum | solution.py:138
  865.9 0.8 fusion.25
  (29 shorter events, 0.4 us)
Async XLA Ops:
  7.2 151.1 %all-gather.5.cloned.1.call-start = ((), (), s32[]{:S(2)}) async-start(), calls=%async_computation.6 | async-start | bytes 4325376 | tf_op jit(solution)/shard_map/all_gather | solution.py:86
  21.4 295.5 %all-gather.9.cloned.1.call-start = ((), (), s32[]{:S(2)}) async-start(), calls=%async_computation.9 | async-start | bytes 4325376 | tf_op jit(solution)/shard_map/all_gather | solution.py:107
  22.2 350.1 %reduce-scatter.3.cloned.1.call-start = ((), (), s32[]{:S(2)}) async-start(), calls=%async_computation.7 | async-start | bytes 1310720 | tf_op jit(solution)/shard_map/reduce_scatter | solution.py:93
  158.2 2.9 copy-start.6
  164.5 293.6 %reduce-scatter.5.cloned.1.call-start = ((), (), s32[]{:S(2)}) async-start(), calls=%async_computation.11 | async-start | bytes 10485760 | tf_op jit(solution)/shard_map/reduce_scatter | solution.py:110
  380.4 0.7 copy-start.5
  380.4 144.8 %all-gather.7.cloned.1.call-start = ((), (), s32[]{:S(2)}) async-start(), calls=%async_computation.8 | async-start | bytes 10485760 | tf_op jit(solution)/shard_map/all_gather | solution.py:100
  458.1 67.1 %copy-start.4 = (bf16[256,512]{1,0:T(8,128)(2,1)S(1)}, bf16[256,512]{1,0:T(8,128)(2,1)}, u32[]{:S(2)}) copy-start(bf16[256,512]{1,0:T(8,128)(2,1)} %reduce-scatter.3.cloned.1.call-done) | copy-start | bytes 786436
  462.8 90.6 %all-gather.11.cloned.1.call-start = ((), (), s32[]{:S(2)}) async-start(), calls=%async_computation.10 | async-start | bytes 1310720 | tf_op jit(solution)/shard_map/all_gather | solution.py:117
  560.7 61.4 %all-to-all-start.2 = ((bf16[32,32,2048]{2,1,0:T(8,128)(2,1)}), bf16[32,32,2048]{2,1,0:T(8,128)(2,1)}, u32[]{:S(2)}, u32[]{:S(2)}) async-start(bf16[32,32,2048]{2,1,0:T(8,128)(2,1)} %bitcast.47), calls=%async_computation.3 | async-start | bytes 8388608 | tf_op jit(solution)/shard_map/all_to_all | solution.py:18
  575.5 56.7 %copy-start.2 = (f32[8192]{0:T(1024)S(1)}, f32[8192]{0:T(1024)}, u32[]{:S(2)}) copy-start(f32[8192]{0:T(1024)} %param.8) | copy-start | bytes 98308
  575.5 56.7 %copy-start = (bf16[1024,512]{1,0:T(8,128)(2,1)S(1)}, bf16[1024,512]{1,0:T(8,128)(2,1)}, u32[]{:S(2)}) copy-start(bf16[1024,512]{1,0:T(8,128)(2,1)} %all-gather.11.cloned.1.call-done) | copy-start | bytes 3145732
  622.0 63.3 %all-to-all-start.1 = ((bf16[32,8,8192]{2,1,0:T(8,128)(2,1)}), bf16[32,8,8192]{2,1,0:T(8,128)(2,1)}, u32[]{:S(2)}, u32[]{:S(2)}) async-start(bf16[32,8,8192]{2,1,0:T(8,128)(2,1)} %fusion), calls=%async_computation.2 | async-start | bytes 8388608 | tf_op jit(solution)/shard_map/all_to_all | solution.py:18
  648.0 48.3 %copy-start.1 = (bf16[8,8192]{1,0:T(8,128)(2,1)S(1)}, bf16[8,8192]{1,0:T(8,128)(2,1)}, u32[]{:S(2)}) copy-start(bf16[8,8192]{1,0:T(8,128)(2,1)} %param.7) | copy-start | bytes 393220
  648.0 217.9 %copy-start.3 = (bf16[8,8192]{1,0:T(8,128)(2,1)S(1)}, bf16[8,8192]{1,0:T(8,128)(2,1)}, u32[]{:S(2)}) copy-start(bf16[8,8192]{1,0:T(8,128)(2,1)} %param.13) | copy-start | bytes 393220
  685.3 10.8 %all-to-all-start.3 = ((bf16[4,8,2048]{2,1,0:T(8,128)(2,1)}), bf16[4,8,2048]{2,1,0:T(8,128)(2,1)S(1)}, u32[]{:S(2)}, u32[]{:S(2)}) async-start(bf16[4,8,2048]{2,1,0:T(8,128)(2,1)} %bitcast.12), calls=%async_computation.4 | async-start | bytes 262144 | tf_op jit(solution)/shard_map/all_to_all | solution.py:133
Sparse Core Ops, SparseCore 0:
  21.6 136.6 all-gather.4
  159.9 157.0 all-gather.8
  320.1 52.1 reduce-scatter.2
  380.5 77.5 reduce-scatter.4
  462.9 62.2 all-gather.6
  533.2 20.1 all-gather.10
